TPU v7x, 32 devices: a whole 2x2x4 slice. The times are simulated.
32 devices in a mesh: grp: 2 (over y), tm: 4 (over z), chan: 4 (over x, core).
Axes of the slice: x: 2, y: 2, z: 4, core: 2. Of those that a mesh axis runs over, the one named last changes fastest.
Arguments:
- voltages: int32 [512, 65536], P(('grp', 'chan'), 'tm'), parts along dimension 0, may hold values from -128 to 127
- beam_delays: int32 [256, 256], replicated, may hold values from 0 to 4095
- cal_gains: float32 [2, 4096, 256], P(None, ('grp', 'tm', 'chan')), parts along dimension 1, may hold values from -4 to 4
Outputs:
- visibilities: bfloat16 [2, 4096, 256, 256], P(None, ('grp', 'tm', 'chan')), parts along dimension 1
- beam_power: bfloat16 [4096, 16, 256], P(('grp', 'tm', 'chan')), parts along dimension 0
There are 2 independent parts, one for each index of `grp`. A program takes and returns all parts, laid end to end along the dimension named above; an argument that names none is the same for every part. Nothing has to cross between parts.
All inputs are finite; a program needn't handle non-finite values.
Results may differ from a plain program's by a relative error of at most 0.0062.
Values may be sent and summed in bfloat16 or wider, within the bound.
A program may use at most 192 MiB of HBM per device.

v0:
```python
import functools
import math

import jax
import jax.numpy as jnp
import numpy as np
from jax import lax
from jax.experimental import pallas as pl
from jax.experimental.pallas import tpu as pltpu
from jax.sharding import PartitionSpec as P

TAPS = 4
FA = 64
FB = 64
NFFT = 4096
CH = 2048


def shifted(block, axis, distance):
    devices = range(lax.axis_size(axis))
    route = [(i - distance, i) for i in devices if i - distance in devices]
    return lax.ppermute(block, axis, route)


def pfb_window():
    total_len = TAPS * NFFT
    sample_pos = jnp.arange(total_len, dtype=jnp.float32)
    centre = (sample_pos - total_len / 2 + 0.5) / NFFT
    taper_win = 0.5 - 0.5 * jnp.cos(2.0 * math.pi * (sample_pos + 0.5) / total_len)
    coeffs = jnp.sinc(centre) * taper_win
    coeffs = coeffs / jnp.sqrt(jnp.sum(coeffs * coeffs))
    return coeffs.reshape(TAPS, NFFT)


RADIX = 32
LANES = NFFT // RADIX


def real_dft(rows):
    size = len(rows)
    if size == 2:
        return [(rows[0] + rows[1], None), (rows[0] - rows[1], None)]
    even, odd = real_dft(rows[0::2]), real_dft(rows[1::2])
    bins = [None] * (size // 2 + 1)
    bins[0] = (even[0][0] + odd[0][0], None)
    bins[size // 2] = (even[0][0] - odd[0][0], None)
    for k in range(1, size // 4):
        cos, sin = math.cos(2 * math.pi * k / size), math.sin(2 * math.pi * k / size)
        o_re, o_im = odd[k]
        t_re = o_re * cos + o_im * sin
        t_im = o_im * cos - o_re * sin
        bins[k] = (even[k][0] + t_re, even[k][1] + t_im)
        bins[size // 2 - k] = (even[k][0] - t_re, t_im - even[k][1])
    bins[size // 4] = (even[size // 4][0], -odd[size // 4][0])
    return bins


def twiddles():
    angle = 2.0 * np.pi * np.outer(np.arange(RADIX // 2 + 1), np.arange(LANES)) / NFFT
    table = np.stack([np.cos(angle), np.sin(angle)], axis=1).astype(np.float32)
    return np.broadcast_to(table[:, :, None, :], table.shape[:2] + (8, LANES))


def second_stage(groups):
    half = LANES // 2
    q = np.arange(LANES)
    angle = 2.0 * np.pi * (np.outer(q, q) % LANES) / LANES
    cos, sin = np.cos(angle) / 64.0, np.sin(angle) / 64.0
    real = np.concatenate([cos, sin], axis=1)
    imag = np.concatenate([-sin, cos], axis=1)
    plain = np.stack([real[:half], imag[:half]])
    mirror = np.stack([real[::-1][:half], -imag[::-1][:half]])
    none = np.zeros_like(plain)

    def ordered(first, second):
        rows = np.stack([first, second]).reshape(2, 2, groups, half // groups, 2 * LANES)
        return rows.transpose(2, 0, 1, 3, 4).reshape(2 * LANES, 2 * LANES)

    full = np.stack([ordered(plain, mirror), ordered(plain, none), ordered(none, plain)])
    high = full.astype(jnp.bfloat16)
    low = (full - high.astype(np.float64)).astype(jnp.bfloat16)
    return np.stack([high, low], axis=1)


def channelize_kernel(volt_ref, halo_ref, window_ref, twiddle_ref, dft_ref, out_ref, late, inner):
    inputs = volt_ref.shape[0]
    spectra = volt_ref.shape[1] // NFFT
    late[...] = halo_ref[...].astype(jnp.float32)

    def filter_rows(group, carry):
        first = pl.multiple_of(group * 8, 8)
        at = pl.ds(first, 8)
        for s in range(spectra):
            pieces = []
            for a in range(RADIX):
                total = None
                for tap in range(TAPS):
                    block = s + tap
                    if block < spectra:
                        col = block * NFFT + a * LANES
                        sample = volt_ref[at, col : col + LANES].astype(jnp.float32)
                    else:
                        col = (block - spectra) * NFFT + a * LANES
                        sample = late[at, col : col + LANES]
                    term = window_ref[tap, :, a * LANES : (a + 1) * LANES] * sample
                    total = term if total is None else total + term
                pieces.append(total)
            to = pl.ds(pl.multiple_of(s * inputs + first, 8), 8)
            for k, (re, im) in enumerate(real_dft(pieces)):
                cos, sin = twiddle_ref[k, 0], twiddle_ref[k, 1]
                if im is None:
                    inner[k, to, :LANES] = re * cos
                    inner[k, to, LANES:] = -re * sin
                else:
                    inner[k, to, :LANES] = re * cos + im * sin
                    inner[k, to, LANES:] = im * cos - re * sin
        return carry

    lax.fori_loop(0, inputs // 8, filter_rows, 0)

    def product(which, bins):
        over = (((1,), (1,)), ((), ()))
        dot = functools.partial(
            lax.dot_general, dimension_numbers=over, preferred_element_type=jnp.float32
        )
        high = bins.astype(jnp.bfloat16)
        low = (bins - high.astype(jnp.float32)).astype(jnp.bfloat16)
        return dot(dft_ref[which, 0], high) + (
            dot(dft_ref[which, 1], high) + dot(dft_ref[which, 0], low)
        )

    out_ref[0] = (product(1, inner[0]) + product(2, inner[RADIX // 2])).astype(jnp.bfloat16)

    def transform_bin(k, carry):
        out_ref[k] = product(0, inner[k]).astype(jnp.bfloat16)
        return carry

    lax.fori_loop(1, RADIX // 2, transform_bin, 0)


def channelize(voltages, halo, groups, **options):
    inputs = voltages.shape[0]
    rows = inputs * (voltages.shape[1] // NFFT)
    window = jnp.broadcast_to(pfb_window()[:, None, :], (TAPS, 8, NFFT))
    return pl.pallas_call(
        channelize_kernel,
        out_shape=jax.ShapeDtypeStruct((RADIX // 2, 2 * LANES, rows), jnp.bfloat16),
        scratch_shapes=[
            pltpu.VMEM(halo.shape, jnp.float32),
            pltpu.VMEM((RADIX // 2 + 1, rows, 2 * LANES), jnp.float32),
        ],
        name="channelize",
        **options,
    )(voltages, halo, window, twiddles(), second_stage(groups))


def correlate_kernel(
    spec_ref, gain_ref, delay_ref, vis_ref, power_ref, cur_re, cur_im, rot_re, rot_im, w_re, w_im
):
    step = pl.program_id(0)
    block = spec_ref.shape[1]
    spectra = spec_ref.shape[2]
    inputs = spec_ref.shape[3]
    beams = delay_ref.shape[0]

    @pl.when(step == 0)
    def _():
        chan_count = lax.axis_size("chan")
        first = (lax.axis_index("tm") * chan_count + lax.axis_index("chan")) * (
            block * pl.num_programs(0)
        )
        delays = delay_ref[...].T
        start = (delays * first % NFFT).astype(jnp.float32) * (2.0 * math.pi / NFFT)
        turn = delays.astype(jnp.float32) * (2.0 * math.pi / NFFT)
        norm = 1.0 / math.sqrt(inputs)
        cur_re[...] = jnp.cos(start) * norm
        cur_im[...] = -jnp.sin(start) * norm
        rot_re[...] = jnp.cos(turn)
        rot_im[...] = -jnp.sin(turn)

    rows = 16

    def advance(chunk, carry):
        at = pl.ds(pl.multiple_of(chunk * rows, rows), rows)
        c_re, c_im = cur_re[at, :], cur_im[at, :]
        r_re, r_im = rot_re[at, :], rot_im[at, :]
        for c in range(block):
            w_re[c, at, :] = c_re.astype(jnp.bfloat16)
            w_im[c, at, :] = c_im.astype(jnp.bfloat16)
            c_re, c_im = c_re * r_re - c_im * r_im, c_re * r_im + c_im * r_re
        cur_re[at, :] = c_re
        cur_im[at, :] = c_im
        return carry

    lax.fori_loop(0, inputs // rows, advance, 0)

    for c in range(block):
        a_re = spec_ref[0, c].astype(jnp.float32)
        a_im = spec_ref[1, c].astype(jnp.float32)
        g_re = gain_ref[0, c : c + 1, :]
        g_im = gain_ref[1, c : c + 1, :]
        cal_re = (g_re * a_re - g_im * a_im).astype(jnp.bfloat16)
        cal_im = (g_re * a_im + g_im * a_re).astype(jnp.bfloat16)
        stacked = jnp.concatenate([cal_re, cal_im], axis=0)
        flipped = jnp.concatenate([cal_im, -cal_re], axis=0)
        over_time = (((0,), (0,)), ((), ()))
        for part, left in enumerate((stacked, flipped)):
            vis = lax.dot_general(left, stacked, over_time, preferred_element_type=jnp.float32)
            vis_ref[part, c] = (vis * (1.0 / spectra)).astype(jnp.bfloat16)
        by_re = jnp.dot(stacked, w_re[c], preferred_element_type=jnp.float32)
        by_im = jnp.dot(stacked, w_im[c], preferred_element_type=jnp.float32)
        beam_re = by_re[:spectra] - by_im[spectra:]
        beam_im = by_re[spectra:] + by_im[:spectra]
        power_ref[c] = (beam_re * beam_re + beam_im * beam_im).astype(jnp.bfloat16)


def correlate(spectra, beam_delays, cal_gains):
    _, chan_local, spectra_total, inputs = spectra.shape
    beams = beam_delays.shape[0]
    block = math.gcd(chan_local, 8)
    table = pltpu.VMEM((inputs, beams), jnp.float32)
    return pl.pallas_call(
        correlate_kernel,
        grid=(chan_local // block,),
        in_specs=[
            pl.BlockSpec((2, block, spectra_total, inputs), lambda g: (0, g, 0, 0)),
            pl.BlockSpec((2, block, inputs), lambda g: (0, g, 0)),
            pl.BlockSpec((beams, inputs), lambda g: (0, 0)),
        ],
        out_specs=[
            pl.BlockSpec((2, block, inputs, inputs), lambda g: (0, g, 0, 0)),
            pl.BlockSpec((block, spectra_total, beams), lambda g: (g, 0, 0)),
        ],
        out_shape=[
            jax.ShapeDtypeStruct((2, chan_local, inputs, inputs), jnp.bfloat16),
            jax.ShapeDtypeStruct((chan_local, spectra_total, beams), jnp.bfloat16),
        ],
        scratch_shapes=[table] * 4 + [pltpu.VMEM((block, inputs, beams), jnp.bfloat16)] * 2,
        compiler_params=pltpu.CompilerParams(dimension_semantics=("arbitrary",)),
        name="correlate",
    )(spectra, cal_gains, beam_delays)


def shards(voltages, beam_delays, cal_gains):
    inp_dev = voltages.shape[0]
    spec_dev = voltages.shape[1] // NFFT
    tm_count = lax.axis_size("tm")
    chan_count = lax.axis_size("chan")
    spectra_total = spec_dev * tm_count
    halo = shifted(voltages[:, : (TAPS - 1) * NFFT].astype(jnp.bfloat16), "tm", -1)
    half = LANES // 2
    bins = channelize(voltages, halo, half).reshape(RADIX // 2, half, 2, 2, spec_dev, inp_dev)
    plain, mirror = bins[:, :, 0], bins[:, :, 1]
    bins = jnp.concatenate([plain, mirror[:1], mirror[:0:-1]], axis=0)
    packed = bins.transpose(2, 1, 0, 3, 4).reshape(2, CH, spec_dev, inp_dev)
    chan_local = CH // (tm_count * chan_count)
    reordered = packed.reshape(2, tm_count, chan_count, chan_local, spec_dev, inp_dev)
    reordered = reordered.transpose(0, 2, 1, 3, 4, 5).reshape(2, CH, spec_dev, inp_dev)
    sectioned = lax.all_to_all(reordered, "chan", split_axis=1, concat_axis=3, tiled=True)
    turned = lax.all_to_all(sectioned, "tm", split_axis=1, concat_axis=2, tiled=True)
    return correlate(turned, beam_delays, cal_gains)


def solution(mesh):
    return jax.shard_map(
        shards,
        mesh=mesh,
        in_specs=(P(("grp", "chan"), "tm"), P(), P(None, ("grp", "tm", "chan"), None)),
        out_specs=(
            P(None, ("grp", "tm", "chan"), None, None),
            P(("grp", "tm", "chan"), None, None),
        ),
        check_vma=False,
    )
```

profile of v0, /device:TPU:0, one launch (start us, length us, event | category | flops | bytes accessed | tf_op | source)
XLA Modules:
  0.0 219.2 jit_solution(13094158814147443805)
XLA Ops:
  0.6 0.0 copy-start.1
  0.6 2.1 slice_convert_fusion
  2.7 1.3 collective-permute-start
  4.0 0.9 fusion.42
  5.6 0.6 fusion.15
  6.3 35.8 %collective-permute-done.halo_ref = bf16[64,12288]{1,0:T(8,128)(2,1)S(1)} collective-permute-done((bf16[64,12288]{1,0:T(8,128)(2,1)S(1)}, bf16[64,12288]{1,0:T(8,128)(2,1)S(1)}, u32[]{:S(2)}, u32[]{:S(2)}) %collective-permute-start) | collective-permute-done | bytes 1572896 | tf_op jit(solution)/shard_map/ppermute | solution.py:22
  42.0 0.0 copy-start
  42.0 0.9 broadcast_in_dim.10.window_ref
  43.0 0.0 copy-done.1
  43.0 0.7 jit_solution_.3.twiddle_ref
  43.6 0.0 copy-done
  43.6 12.4 %channelize.1 = bf16[16,256,256]{2,1,0:T(8,128)(2,1)} custom-call(s32[64,16384]{1,0:T(8,128)} %volt_ref.1, bf16[64,12288]{1,0:T(8,128)(2,1)} %copy-done, f32[4,8,4096]{2,1,0:T(8,128)} %broadcast_in_dim.10.window_ref, f32[17,2,8,128]{3,2,1,0:T(8,128)} %jit_solution_.3.twiddle_ref, bf16[3,2,256,256]{3,2,1,0:T(8,128)(2,1)} %constant.69.clone.dft_ref), custom_call_target="tpu_custom_call" | custom-call | tf_op jit(solution)/shard_map/channelize/pallas_call | solution.py:145
  56.0 7.1 %reshape.62 = bf16[16,64,2,2,4,64]{5,4,3,2,1,0:T(4,128)(2,1)} reshape(bf16[16,256,256]{2,1,0:T(8,128)(2,1)} %channelize.1) | data formatting | bytes 4194304 | tf_op jit(solution)/shard_map/reshape | solution.py:252
  63.1 0.9 slice.30
  64.0 2.3 %slice.31 = bf16[15,64,1,2,4,64]{5,4,3,2,1,0:T(4,128)(2,1)S(1)} slice(bf16[16,64,2,2,4,64]{5,4,3,2,1,0:T(4,128)(2,1)} %reshape.62), slice={[1:16], [0:64], [1:2], [0:2], [0:4], [0:64]} | slice | bytes 1966080 | tf_op jit(solution)/shard_map/slice | solution.py:254
  66.3 0.0 slice-start
  66.4 0.2 copy.34
  66.6 1.3 slice-done
  67.9 2.7 %copy.53 = bf16[16,64,1,2,4,64]{5,0,1,4,3,2:T(8,128)(2,1)} copy(bf16[16,64,1,2,4,64]{5,4,3,2,1,0:T(4,128)(2,1)S(1)} %slice-done) | data formatting | bytes 2097152
  70.6 1.3 copy.52
  71.9 4.0 %rev.3 = bf16[15,64,2,4,64]{4,0,1,3,2:T(8,128)(2,1)} reverse(bf16[15,64,2,4,64]{4,0,1,3,2:T(8,128)(2,1)S(1)} %bitcast.29), dimensions={0} | reverse | bytes 1966080 | tf_op jit(solution)/shard_map/rev | solution.py:254
  75.9 3.5 %pad_maximum_fusion = bf16[32,64,2,4,64]{4,0,1,3,2:T(8,128)(2,1)S(1)} fusion(bf16[15,64,2,4,64]{4,0,1,3,2:T(8,128)(2,1)} %rev.3, bf16[1,64,2,4,64]{4,0,1,3,2:T(2,128)(2,1)S(1)} %copy.34, bf16[16,64,2,4,64]{4,0,1,3,2:T(8,128)(2,1)} %bitcast.31), kind=kLoop, calls=%fused_computation | loop fusion | flops 6291456 | bytes 4194304 | tf_op jit(solution)/shard_map/concatenate | solution.py:254
  79.4 5.5 %copy.42 = bf16[2,4,4,128,4,64]{5,4,0,3,2,1:T(4,128)(2,1)} copy(bf16[2,4,4,128,4,64]{5,3,1,2,4,0:T(8,128)(2,1)S(1)} %bitcast.26) | data formatting | bytes 4194304 | tf_op jit(solution)/shard_map/reshape | solution.py:258
  84.9 4.9 %reshape.64 = bf16[4,2,131072]{2,1,0:T(2,128)(2,1)S(1)} reshape(bf16[2048,2,4,64]{3,2,1,0:T(4,128)(2,1)} %bitcast.27) | data formatting | bytes 4194304
  89.9 28.9 %all_to_all.36 = bf16[4,2,131072]{2,1,0:T(2,128)(2,1)} all-to-all(bf16[4,2,131072]{2,1,0:T(2,128)(2,1)S(1)} %reshape.64), channel_id=1, replica_groups=mesh['grp'=2,'tm'=4,'chan'=4] {'chan'}, dimensions={0} | all-to-all | bytes 4194304 | tf_op jit(solution)/shard_map/all_to_all | solution.py:259
  118.8 5.8 %reshape.65 = bf16[2048,2,4,64]{3,2,1,0:T(4,128)(2,1)} reshape(bf16[4,2,131072]{2,1,0:T(2,128)(2,1)} %all_to_all.36) | data formatting | bytes 4194304
  124.6 5.6 %copy.38 = bf16[2,512,4,4,64]{1,4,3,2,0:T(8,128)(2,1)S(1)} copy(bf16[2,512,4,4,64]{4,2,0,1,3:T(4,128)(2,1)} %bitcast.25) | data formatting | bytes 4194304 | tf_op jit(solution)/shard_map/all_to_all | solution.py:259
  130.2 3.1 %copy.39 = bf16[2,512,4,256]{3,2,0,1:T(4,128)(2,1)} copy(bf16[2,512,4,256]{1,3,2,0:T(8,128)(2,1)S(1)} %bitcast.28) | data formatting | bytes 4194304 | tf_op jit(solution)/shard_map/all_to_all | solution.py:259
  133.2 51.8 %all_to_all.37 = bf16[2,512,4,256]{3,2,0,1:T(4,128)(2,1)S(1)} all-to-all(bf16[2,512,4,256]{3,2,0,1:T(4,128)(2,1)} %copy.39), channel_id=1, replica_groups=mesh['grp'=2,'tm'=4,'chan'=4] {'tm'}, dimensions={1} | all-to-all | bytes 4194304 | tf_op jit(solution)/shard_map/all_to_all | solution.py:260
  185.1 0.4 copy.40
  185.5 1.6 copy.41
  187.1 2.1 all_to_all.33.spec_ref
  189.2 30.0 %correlate.1 = (bf16[2,128,256,256]{3,2,1,0:T(8,128)(2,1)}, bf16[128,16,256]{2,1,0:T(8,128)(2,1)}) custom-call(bf16[2,128,16,256]{3,2,1,0:T(8,128)(2,1)} %all_to_all.33.spec_ref, f32[2,128,256]{2,1,0:T(8,128)} %gain_ref.1, s32[256,256]{1,0:T(8,128)} %delay_ref.1), custom_call_target="tpu_custom_call" | custom-call | tf_op jit(solution)/shard_map/correlate/pallas_call | solution.py:222
  (1 shorter events, 0.0 us)
Async XLA Ops:
  0.6 42.3 %copy-start.1 = (f32[17,2,128]{2,1,0:T(2,128)S(1)}, f32[17,2,128]{2,1,0:T(2,128)}, u32[]{:S(2)}) copy-start(f32[17,2,128]{2,1,0:T(2,128)} %constant.68.clone) | copy-start | bytes 52228
  2.7 39.3 %collective-permute-start = (bf16[64,12288]{1,0:T(8,128)(2,1)S(1)}, bf16[64,12288]{1,0:T(8,128)(2,1)S(1)}, u32[]{:S(2)}, u32[]{:S(2)}) collective-permute-start(bf16[64,12288]{1,0:T(8,128)(2,1)S(1)} %slice_convert_fusion), channel_id=1, source_target_pairs={{4,0},{8,4},{12,8},{5,1},{9,5},{13,9},{6,2},{10,6},{14,10},{7,3},{... | collective-permute-start | bytes 4718600 | tf_op jit(solution)/shard_map/ppermute | solution.py:22
  42.0 1.6 copy-start
  66.3 1.6 slice-start
where the time goes:
time: 220 us; the launch traced here: 219 us
  blocking collectives  80.7 us (37%)
  local copies, waits for them, and re-layouts  50.4 us (23%)
  Pallas kernels  42.4 us (19%)
  waiting for transfers between devices  35.8 us (16%)
  other arithmetic  7.16 us (3%)
    all_to_all x1, blocking collectives, shards(): lax.all_to_all(sectioned, 'tm', split_axis=1, concat_axis=2, tiled=True)  51.8 us
    ppermute x1, waiting for transfers between devices, shifted(): return lax.ppermute(block, axis, route)  35.8 us
    pallas_call x1, Pallas kernels, correlate(): pl.pallas_call(correlate_kernel, grid=(chan_local // block,), in_specs=[p...  30 us
    all_to_all x1, blocking collectives, shards(): lax.all_to_all(reordered, 'chan', split_axis=1, concat_axis=3, tiled=True)  28.9 us
    unnamed x9, local copies, waits for them, and re-layouts  14.7 us
    pallas_call x1, Pallas kernels, channelize(): pl.pallas_call(channelize_kernel, out_shape=jax.ShapeDtypeStruct((RADIX /...  12.4 us
    all_to_all x2, local copies, waits for them, and re-layouts, shards(): lax.all_to_all(reordered, 'chan', split_axis=1, concat_axis=3, tiled=True)  8.65 us
    reshape x1, local copies, waits for them, and re-layouts, shards(): channelize(voltages, halo, half)  7.06 us
  transfers between devices with their start and end apart: 1, of which 1 were waited for; matrix products, arithmetic and copies ran while one was open for 1% of the time, Pallas kernels for 0%

commit v1 on v0

--- a/solution.py
+++ b/solution.py
@@ -129,29 +129,222 @@
             dot(dft_ref[which, 1], high) + dot(dft_ref[which, 0], low)
         )
 
-    out_ref[0] = (product(1, inner[0]) + product(2, inner[RADIX // 2])).astype(jnp.bfloat16)
+    def put(k, value):
+        groups, _, size, lanes = out_ref.shape
+        out_ref[:, k] = value.astype(jnp.bfloat16).reshape(groups, size, lanes)
+
+    put(0, product(1, inner[0]) + product(2, inner[RADIX // 2]))
 
     def transform_bin(k, carry):
-        out_ref[k] = product(0, inner[k]).astype(jnp.bfloat16)
+        put(k, product(0, inner[k]))
         return carry
 
     lax.fori_loop(1, RADIX // 2, transform_bin, 0)
 
 
-def channelize(voltages, halo, groups, **options):
+def channelize(voltages, halo, groups):
     inputs = voltages.shape[0]
     rows = inputs * (voltages.shape[1] // NFFT)
     window = jnp.broadcast_to(pfb_window()[:, None, :], (TAPS, 8, NFFT))
     return pl.pallas_call(
         channelize_kernel,
-        out_shape=jax.ShapeDtypeStruct((RADIX // 2, 2 * LANES, rows), jnp.bfloat16),
+        out_shape=jax.ShapeDtypeStruct(
+            (groups, RADIX // 2, 2 * LANES // groups, rows), jnp.bfloat16
+        ),
         scratch_shapes=[
             pltpu.VMEM(halo.shape, jnp.float32),
             pltpu.VMEM((RADIX // 2 + 1, rows, 2 * LANES), jnp.float32),
         ],
         name="channelize",
-        **options,
     )(voltages, halo, window, twiddles(), second_stage(groups))
+
+
+def exchange_kernel(out_ref, in_ref, send_sems, recv_sems, own_sem):
+    tm_count, chan_count = lax.axis_size("tm"), lax.axis_size("chan")
+    tm, chan = lax.axis_index("tm"), lax.axis_index("chan")
+    slot = chan * tm_count + tm
+    peers = []
+    for tm_step in range(tm_count):
+        for chan_step in range(chan_count):
+            peer_tm = lax.rem(tm + tm_step, tm_count)
+            peer_chan = lax.rem(chan + chan_step, chan_count)
+            if tm_step or chan_step:
+                peers.append((peer_tm, peer_chan))
+    barrier = pltpu.get_barrier_semaphore()
+    for peer_tm, peer_chan in peers:
+        pl.semaphore_signal(
+            barrier,
+            inc=1,
+            device_id={"tm": peer_tm, "chan": peer_chan},
+            device_id_type=pl.DeviceIdType.MESH,
+        )
+    pl.semaphore_wait(barrier, len(peers))
+    copies = []
+    for index, (peer_tm, peer_chan) in enumerate(peers):
+        copy = pltpu.make_async_remote_copy(
+            src_ref=out_ref.at[peer_tm * chan_count + peer_chan],
+            dst_ref=in_ref.at[slot],
+            send_sem=send_sems.at[index],
+            recv_sem=recv_sems.at[index],
+            device_id={"tm": peer_tm, "chan": peer_chan},
+            device_id_type=pl.DeviceIdType.MESH,
+        )
+        copy.start()
+        copies.append(copy)
+    own = pltpu.make_async_copy(out_ref.at[tm * chan_count + chan], in_ref.at[slot], own_sem)
+    own.start()
+    own.wait()
+    for copy in copies:
+        copy.wait()
+
+
+def exchange(bins):
+    return pl.pallas_call(
+        exchange_kernel,
+        in_specs=[pl.BlockSpec(memory_space=pl.ANY)],
+        out_specs=pl.BlockSpec(memory_space=pl.ANY),
+        out_shape=jax.ShapeDtypeStruct(bins.shape, bins.dtype),
+        scratch_shapes=[
+            pltpu.SemaphoreType.DMA((bins.shape[0] - 1,)),
+            pltpu.SemaphoreType.DMA((bins.shape[0] - 1,)),
+            pltpu.SemaphoreType.DMA,
+        ],
+        compiler_params=pltpu.CompilerParams(collective_id=0, has_side_effects=True),
+        name="exchange",
+    )(bins)
+
+
+def correlate_bins_kernel(
+    bins_ref, gain_ref, delay_ref, vis_ref, power_ref,
+    cur_re, cur_im, rot_re, rot_im, far_re, far_im, w_re, w_im, rows_buf, power_buf,
+):
+    k1 = pl.program_id(0)
+    tm_count, chan_count = lax.axis_size("tm"), lax.axis_size("chan")
+    sources, _, size, lanes = bins_ref.shape
+    block = vis_ref.shape[1]
+    inputs = vis_ref.shape[4]
+    own_inputs = inputs // chan_count
+    spec_dev = lanes // own_inputs
+    spectra = spec_dev * tm_count
+
+    @pl.when(k1 == 0)
+    def _():
+        first = (lax.axis_index("tm") * chan_count + lax.axis_index("chan")) * (block * RADIX)
+        delays = delay_ref[...].T
+        norm = 1.0 / math.sqrt(inputs)
+
+        def phase(steps):
+            return (delays * steps % NFFT).astype(jnp.float32) * (2.0 * math.pi / NFFT)
+
+        cur_re[...] = jnp.cos(phase(first)) * norm
+        cur_im[...] = -jnp.sin(phase(first)) * norm
+        rot_re[...] = jnp.cos(phase(1))
+        rot_im[...] = -jnp.sin(phase(1))
+        far_re[...] = jnp.cos(phase(RADIX))
+        far_im[...] = -jnp.sin(phase(RADIX))
+
+    rows = 16
+
+    def advance(chunk, carry):
+        at = pl.ds(pl.multiple_of(chunk * rows, rows), rows)
+        c_re, c_im = cur_re[at, :], cur_im[at, :]
+        r_re, r_im = rot_re[at, :], rot_im[at, :]
+        cur_re[at, :] = c_re * r_re - c_im * r_im
+        cur_im[at, :] = c_re * r_im + c_im * r_re
+        r_re, r_im = far_re[at, :], far_im[at, :]
+        for q in range(block):
+            w_re[q, at, :] = c_re.astype(jnp.bfloat16)
+            w_im[q, at, :] = c_im.astype(jnp.bfloat16)
+            if q + 1 < block:
+                c_re, c_im = c_re * r_re - c_im * r_im, c_re * r_im + c_im * r_re
+        return carry
+
+    lax.fori_loop(0, inputs // rows, advance, 0)
+
+    received = bins_ref[...].astype(jnp.float32).reshape(sources * size, lanes)
+    for part in range(lanes // LANES):
+        rows_buf[part] = received[:, part * LANES : (part + 1) * LANES]
+    mirror = jnp.where(k1 >= RADIX // 2, size // 2, 0)
+
+    def gathered(row):
+        parts = []
+        for chan in range(chan_count):
+            at = pl.ds(chan * tm_count * size + mirror + row, tm_count, stride=size)
+            pieces = [rows_buf[part, at, :] for part in range(lanes // LANES)]
+            parts.append(jnp.concatenate(pieces, axis=1))
+        return jnp.concatenate(
+            [
+                jnp.concatenate([p[:, s * own_inputs : (s + 1) * own_inputs] for p in parts], axis=1)
+                for s in range(spec_dev)
+            ],
+            axis=0,
+        )
+
+    g_re_all, g_im_all = gain_ref[0, :, 0], gain_ref[1, :, 0]
+    for q in range(block):
+        a_re, a_im = gathered(q), gathered(block + q)
+        g_re, g_im = g_re_all[q], g_im_all[q]
+        cal_re = (g_re * a_re - g_im * a_im).astype(jnp.bfloat16)
+        cal_im = (g_re * a_im + g_im * a_re).astype(jnp.bfloat16)
+        stacked = jnp.concatenate([cal_re, cal_im], axis=0)
+        flipped = jnp.concatenate([cal_im, -cal_re], axis=0)
+        over_time = (((0,), (0,)), ((), ()))
+        for part, left in enumerate((stacked, flipped)):
+            vis = lax.dot_general(left, stacked, over_time, preferred_element_type=jnp.float32)
+            vis_ref[part, q, 0] = (vis * (1.0 / spectra)).astype(jnp.bfloat16)
+        by_re = jnp.dot(stacked, w_re[q], preferred_element_type=jnp.float32)
+        by_im = jnp.dot(stacked, w_im[q], preferred_element_type=jnp.float32)
+        beam_re = by_re[:spectra] - by_im[spectra:]
+        beam_im = by_re[spectra:] + by_im[:spectra]
+        power = beam_re * beam_re + beam_im * beam_im
+        for part in range(power.shape[1] // LANES):
+            cols = slice(part * LANES, (part + 1) * LANES)
+            power_buf[q, part] = power[:, cols]
+            in_order = [
+                power_buf[q, part, pl.ds(t, spec_dev, stride=tm_count), :] for t in range(tm_count)
+            ]
+            power_ref[q, 0, :, cols] = jnp.concatenate(in_order, axis=0).astype(jnp.bfloat16)
+
+
+def correlate_bins(bins, beam_delays, cal_gains):
+    sources, half, size, lanes = bins.shape
+    _, chan_local, inputs = cal_gains.shape
+    beams = beam_delays.shape[0]
+    block = chan_local // RADIX
+    spectra = sources * lanes // inputs
+    table = pltpu.VMEM((inputs, beams), jnp.float32)
+    vis, power = pl.pallas_call(
+        correlate_bins_kernel,
+        grid=(RADIX,),
+        in_specs=[
+            pl.BlockSpec(
+                (sources, 1, size, lanes),
+                lambda k: (0, jnp.where(k > half, RADIX - k, lax.rem(k, half)), 0, 0),
+            ),
+            pl.BlockSpec((2, block, 1, 1, inputs), lambda k: (0, 0, k, 0, 0)),
+            pl.BlockSpec((beams, inputs), lambda k: (0, 0)),
+        ],
+        out_specs=[
+            pl.BlockSpec((2, block, 1, inputs, inputs), lambda k: (0, 0, k, 0, 0)),
+            pl.BlockSpec((block, 1, spectra, beams), lambda k: (0, k, 0, 0)),
+        ],
+        out_shape=[
+            jax.ShapeDtypeStruct((2, block, RADIX, inputs, inputs), jnp.bfloat16),
+            jax.ShapeDtypeStruct((block, RADIX, spectra, beams), jnp.bfloat16),
+        ],
+        scratch_shapes=[table] * 6
+        + [pltpu.VMEM((block, inputs, beams), jnp.bfloat16)] * 2
+        + [
+            pltpu.VMEM((lanes // LANES, sources * size, LANES), jnp.float32),
+            pltpu.VMEM((block, beams // LANES, spectra, LANES), jnp.float32),
+        ],
+        compiler_params=pltpu.CompilerParams(dimension_semantics=("arbitrary",)),
+        name="correlate",
+    )(bins, cal_gains.reshape(2, block, RADIX, 1, inputs), beam_delays)
+    return (
+        vis.reshape(2, chan_local, inputs, inputs),
+        power.reshape(chan_local, spectra, beams),
+    )
 
 
 def correlate_kernel(
@@ -248,6 +441,10 @@
     chan_count = lax.axis_size("chan")
     spectra_total = spec_dev * tm_count
     halo = shifted(voltages[:, : (TAPS - 1) * NFFT].astype(jnp.bfloat16), "tm", -1)
+    devices = tm_count * chan_count
+    if CH % (4 * RADIX * devices) == 0:
+        bins = exchange(channelize(voltages, halo, devices))
+        return correlate_bins(bins, beam_delays, cal_gains)
     half = LANES // 2
     bins = channelize(voltages, halo, half).reshape(RADIX // 2, half, 2, 2, spec_dev, inp_dev)
     plain, mirror = bins[:, :, 0], bins[:, :, 1]

time: 220 us -> 149 us (0.68)
  the two profiles are of different devices: /device:TPU:0 before, /device:TPU:9 now
where the time goes in v1:
time: 149 us; the launch traced here: 148 us
  Pallas kernels  107 us (72%)
  waiting for transfers between devices  32 us (21%)
  other arithmetic  3.66 us (2%)
  local copies, waits for them, and re-layouts  2.54 us (2%)
  starting transfers between devices  1.92 us (1%)
    pallas_call x1, Pallas kernels, exchange(): pl.pallas_call(exchange_kernel, in_specs=[pl.BlockSpec(memory_space=pl.AN...  50.5 us
    pallas_call x1, Pallas kernels, correlate_bins(): pl.pallas_call(correlate_bins_kernel, grid=(RADIX,), in_specs=[pl.BlockSp...  44.1 us
    ppermute x1, waiting for transfers between devices, shifted(): return lax.ppermute(block, axis, route)  32 us
    pallas_call x1, Pallas kernels, channelize(): pl.pallas_call(channelize_kernel, out_shape=jax.ShapeDtypeStruct((groups,...  12.4 us
  transfers between devices with their start and end apart: 1, of which 1 were waited for; matrix products, arithmetic and copies ran while one was open for 2% of the time, Pallas kernels for 0%

profile of v1, /device:TPU:9, one launch (start us, length us, event | category | flops | bytes accessed | tf_op | source)
XLA Modules:
  0.0 148.4 jit_solution(12148946496644832711)
XLA Ops:
  0.6 0.0 copy-start.2
  0.6 0.0 copy-start.1
  0.7 2.1 %slice_convert_fusion = bf16[64,12288]{1,0:T(8,128)(2,1)S(1)} fusion(s32[64,16384]{1,0:T(8,128)} %volt_ref.1), kind=kLoop, calls=%fused_computation | loop fusion | flops 786432 | bytes 4718592 | tf_op jit(solution)/shard_map/convert
  2.7 1.9 %collective-permute-start = (bf16[64,12288]{1,0:T(8,128)(2,1)S(1)}, bf16[64,12288]{1,0:T(8,128)(2,1)S(1)}, u32[]{:S(2)}, u32[]{:S(2)}) collective-permute-start(bf16[64,12288]{1,0:T(8,128)(2,1)S(1)} %slice_convert_fusion), channel_id=1, source_target_pairs={{4,0},{8,4},{12,8},{5,1},{9,5},{13,9},{6,2},{10,6},{14,10},{7,3},{... | collective-permute-start | bytes 4718600 | tf_op jit(solution)/shard_map/ppermute | solution.py:22
  4.7 0.9 fusion.42
  6.3 0.0 copy-done.1
  6.3 1.0 reshape.63.gain_ref
  7.3 0.6 fusion.15
  7.9 32.0 %collective-permute-done.halo_ref = bf16[64,12288]{1,0:T(8,128)(2,1)S(1)} collective-permute-done((bf16[64,12288]{1,0:T(8,128)(2,1)S(1)}, bf16[64,12288]{1,0:T(8,128)(2,1)S(1)}, u32[]{:S(2)}, u32[]{:S(2)}) %collective-permute-start) | collective-permute-done | bytes 1572896 | tf_op jit(solution)/shard_map/ppermute | solution.py:22
  39.9 0.0 copy-start
  39.9 0.9 broadcast_in_dim.10.window_ref
  40.8 0.0 copy-done.2
  40.8 0.7 jit_solution_.3.twiddle_ref
  41.5 0.0 copy-done
  41.5 12.4 %channelize.1.out_ref = bf16[16,16,16,256]{3,2,1,0:T(8,128)(2,1)} custom-call(s32[64,16384]{1,0:T(8,128)} %volt_ref.1, bf16[64,12288]{1,0:T(8,128)(2,1)} %copy-done, f32[4,8,4096]{2,1,0:T(8,128)} %broadcast_in_dim.10.window_ref, f32[17,2,8,128]{3,2,1,0:T(8,128)} %jit_solution_.3.twiddle_ref, bf16[3,2,256,256]{3,2,1,0:T(8,128)(2,1)} %constant.69.clone.dft_ref), custom_call_target="tpu_custom_call" | custom-call | tf_op jit(solution)/shard_map/channelize/pallas_call | solution.py:149
  53.8 50.5 %exchange.1.bins_ref = bf16[16,16,16,256]{3,2,1,0:T(8,128)(2,1)} custom-call(bf16[16,16,16,256]{3,2,1,0:T(8,128)(2,1)} %channelize.1.out_ref), custom_call_target="tpu_custom_call" | custom-call | tf_op jit(solution)/shard_map/exchange/pallas_call | solution.py:202
  104.3 44.1 %correlate.1 = (bf16[2,4,32,256,256]{4,3,2,1,0:T(8,128)(2,1)}, bf16[4,32,16,256]{3,2,1,0:T(8,128)(2,1)}) custom-call(bf16[16,16,16,256]{3,2,1,0:T(8,128)(2,1)} %exchange.1.bins_ref, f32[2,4,32,1,256]{4,3,2,1,0:T(1,128)} %reshape.63.gain_ref, s32[256,256]{1,0:T(8,128)} %delay_ref.1), custom_call_target="tpu_custom_call" | custom-call | tf_op jit(solution)/shard_map/correlate/pallas_call | solution.py:316
Async XLA Ops:
  0.6 40.2 %copy-start.2 = (f32[17,2,128]{2,1,0:T(2,128)S(1)}, f32[17,2,128]{2,1,0:T(2,128)}, u32[]{:S(2)}) copy-start(f32[17,2,128]{2,1,0:T(2,128)} %constant.68.clone) | copy-start | bytes 52228
  0.6 5.7 %copy-start.1 = (f32[2,128,256]{2,1,0:T(8,128)S(1)}, f32[2,128,256]{2,1,0:T(8,128)}, u32[]{:S(2)}) copy-start(f32[2,128,256]{2,1,0:T(8,128)} %param.7) | copy-start | bytes 786436
  2.7 37.2 %collective-permute-start = (bf16[64,12288]{1,0:T(8,128)(2,1)S(1)}, bf16[64,12288]{1,0:T(8,128)(2,1)S(1)}, u32[]{:S(2)}, u32[]{:S(2)}) collective-permute-start(bf16[64,12288]{1,0:T(8,128)(2,1)S(1)} %slice_convert_fusion), channel_id=1, source_target_pairs={{4,0},{8,4},{12,8},{5,1},{9,5},{13,9},{6,2},{10,6},{14,10},{7,3},{... | collective-permute-start | bytes 4718600 | tf_op jit(solution)/shard_map/ppermute | solution.py:22
  39.9 1.5 %copy-start = (bf16[64,12288]{1,0:T(8,128)(2,1)}, bf16[64,12288]{1,0:T(8,128)(2,1)S(1)}, u32[]{:S(2)}) copy-start(bf16[64,12288]{1,0:T(8,128)(2,1)S(1)} %collective-permute-done.halo_ref) | copy-start | bytes 4718596

commit v2 on v1

--- a/solution.py
+++ b/solution.py
@@ -214,9 +214,67 @@
     )(bins)
 
 
+def weights_kernel(delay_ref, out_ref, cur_re, cur_im, rot_re, rot_im, far_re, far_im):
+    k1 = pl.program_id(0)
+    block = out_ref.shape[1]
+    inputs = out_ref.shape[3]
+
+    @pl.when(k1 == 0)
+    def _():
+        device = lax.axis_index("tm") * lax.axis_size("chan") + lax.axis_index("chan")
+        first = device * (block * RADIX)
+        delays = delay_ref[...].T
+        norm = 1.0 / math.sqrt(inputs)
+
+        def phase(steps):
+            return (delays * steps % NFFT).astype(jnp.float32) * (2.0 * math.pi / NFFT)
+
+        cur_re[...] = jnp.cos(phase(first)) * norm
+        cur_im[...] = -jnp.sin(phase(first)) * norm
+        rot_re[...] = jnp.cos(phase(1))
+        rot_im[...] = -jnp.sin(phase(1))
+        far_re[...] = jnp.cos(phase(RADIX))
+        far_im[...] = -jnp.sin(phase(RADIX))
+
+    rows = 16
+
+    def advance(chunk, carry):
+        at = pl.ds(pl.multiple_of(chunk * rows, rows), rows)
+        c_re, c_im = cur_re[at, :], cur_im[at, :]
+        r_re, r_im = rot_re[at, :], rot_im[at, :]
+        cur_re[at, :] = c_re * r_re - c_im * r_im
+        cur_im[at, :] = c_re * r_im + c_im * r_re
+        r_re, r_im = far_re[at, :], far_im[at, :]
+        for q in range(block):
+            out_ref[0, q, 0, at, :] = c_re.astype(jnp.bfloat16)
+            out_ref[0, q, 1, at, :] = c_im.astype(jnp.bfloat16)
+            if q + 1 < block:
+                c_re, c_im = c_re * r_re - c_im * r_im, c_re * r_im + c_im * r_re
+        return carry
+
+    lax.fori_loop(0, inputs // rows, advance, 0)
+
+
+def beam_weights(beam_delays, block):
+    beams, inputs = beam_delays.shape
+    shape = (RADIX, block, 2, inputs, beams)
+    return pl.pallas_call(
+        weights_kernel,
+        grid=(RADIX,),
+        in_specs=[pl.BlockSpec((beams, inputs), lambda k: (0, 0))],
+        out_specs=pl.BlockSpec((1,) + shape[1:], lambda k: (k, 0, 0, 0, 0)),
+        out_shape=jax.ShapeDtypeStruct(shape, jnp.bfloat16),
+        scratch_shapes=[pltpu.VMEM((inputs, beams), jnp.float32)] * 6,
+        compiler_params=pltpu.CompilerParams(dimension_semantics=("arbitrary",)),
+        cost_estimate=pl.CostEstimate(
+            flops=12 * math.prod(shape), bytes_accessed=2 * math.prod(shape), transcendentals=0
+        ),
+        name="beam_weights",
+    )(beam_delays)
+
+
 def correlate_bins_kernel(
-    bins_ref, gain_ref, delay_ref, vis_ref, power_ref,
-    cur_re, cur_im, rot_re, rot_im, far_re, far_im, w_re, w_im, rows_buf, power_buf,
+    bins_ref, gain_ref, weight_ref, vis_ref, power_ref, rows_buf, power_buf
 ):
     k1 = pl.program_id(0)
     tm_count, chan_count = lax.axis_size("tm"), lax.axis_size("chan")
@@ -226,40 +284,6 @@
     own_inputs = inputs // chan_count
     spec_dev = lanes // own_inputs
     spectra = spec_dev * tm_count
-
-    @pl.when(k1 == 0)
-    def _():
-        first = (lax.axis_index("tm") * chan_count + lax.axis_index("chan")) * (block * RADIX)
-        delays = delay_ref[...].T
-        norm = 1.0 / math.sqrt(inputs)
-
-        def phase(steps):
-            return (delays * steps % NFFT).astype(jnp.float32) * (2.0 * math.pi / NFFT)
-
-        cur_re[...] = jnp.cos(phase(first)) * norm
-        cur_im[...] = -jnp.sin(phase(first)) * norm
-        rot_re[...] = jnp.cos(phase(1))
-        rot_im[...] = -jnp.sin(phase(1))
-        far_re[...] = jnp.cos(phase(RADIX))
-        far_im[...] = -jnp.sin(phase(RADIX))
-
-    rows = 16
-
-    def advance(chunk, carry):
-        at = pl.ds(pl.multiple_of(chunk * rows, rows), rows)
-        c_re, c_im = cur_re[at, :], cur_im[at, :]
-        r_re, r_im = rot_re[at, :], rot_im[at, :]
-        cur_re[at, :] = c_re * r_re - c_im * r_im
-        cur_im[at, :] = c_re * r_im + c_im * r_re
-        r_re, r_im = far_re[at, :], far_im[at, :]
-        for q in range(block):
-            w_re[q, at, :] = c_re.astype(jnp.bfloat16)
-            w_im[q, at, :] = c_im.astype(jnp.bfloat16)
-            if q + 1 < block:
-                c_re, c_im = c_re * r_re - c_im * r_im, c_re * r_im + c_im * r_re
-        return carry
-
-    lax.fori_loop(0, inputs // rows, advance, 0)
 
     received = bins_ref[...].astype(jnp.float32).reshape(sources * size, lanes)
     for part in range(lanes // LANES):
@@ -281,6 +305,7 @@
         )
 
     g_re_all, g_im_all = gain_ref[0, :, 0], gain_ref[1, :, 0]
+    ready = []
     for q in range(block):
         a_re, a_im = gathered(q), gathered(block + q)
         g_re, g_im = g_re_all[q], g_im_all[q]
@@ -288,12 +313,14 @@
         cal_im = (g_re * a_im + g_im * a_re).astype(jnp.bfloat16)
         stacked = jnp.concatenate([cal_re, cal_im], axis=0)
         flipped = jnp.concatenate([cal_im, -cal_re], axis=0)
-        over_time = (((0,), (0,)), ((), ()))
+        ready.append((stacked, flipped))
+    over_time = (((0,), (0,)), ((), ()))
+    for q, (stacked, flipped) in enumerate(ready):
         for part, left in enumerate((stacked, flipped)):
             vis = lax.dot_general(left, stacked, over_time, preferred_element_type=jnp.float32)
             vis_ref[part, q, 0] = (vis * (1.0 / spectra)).astype(jnp.bfloat16)
-        by_re = jnp.dot(stacked, w_re[q], preferred_element_type=jnp.float32)
-        by_im = jnp.dot(stacked, w_im[q], preferred_element_type=jnp.float32)
+        by_re = jnp.dot(stacked, weight_ref[0, q, 0], preferred_element_type=jnp.float32)
+        by_im = jnp.dot(stacked, weight_ref[0, q, 1], preferred_element_type=jnp.float32)
         beam_re = by_re[:spectra] - by_im[spectra:]
         beam_im = by_re[spectra:] + by_im[:spectra]
         power = beam_re * beam_re + beam_im * beam_im
@@ -306,13 +333,12 @@
             power_ref[q, 0, :, cols] = jnp.concatenate(in_order, axis=0).astype(jnp.bfloat16)
 
 
-def correlate_bins(bins, beam_delays, cal_gains):
+def correlate_bins(bins, weights, cal_gains):
     sources, half, size, lanes = bins.shape
     _, chan_local, inputs = cal_gains.shape
-    beams = beam_delays.shape[0]
+    beams = weights.shape[4]
     block = chan_local // RADIX
     spectra = sources * lanes // inputs
-    table = pltpu.VMEM((inputs, beams), jnp.float32)
     vis, power = pl.pallas_call(
         correlate_bins_kernel,
         grid=(RADIX,),
@@ -322,7 +348,7 @@
                 lambda k: (0, jnp.where(k > half, RADIX - k, lax.rem(k, half)), 0, 0),
             ),
             pl.BlockSpec((2, block, 1, 1, inputs), lambda k: (0, 0, k, 0, 0)),
-            pl.BlockSpec((beams, inputs), lambda k: (0, 0)),
+            pl.BlockSpec((1, block, 2, inputs, beams), lambda k: (k, 0, 0, 0, 0)),
         ],
         out_specs=[
             pl.BlockSpec((2, block, 1, inputs, inputs), lambda k: (0, 0, k, 0, 0)),
@@ -332,15 +358,13 @@
             jax.ShapeDtypeStruct((2, block, RADIX, inputs, inputs), jnp.bfloat16),
             jax.ShapeDtypeStruct((block, RADIX, spectra, beams), jnp.bfloat16),
         ],
-        scratch_shapes=[table] * 6
-        + [pltpu.VMEM((block, inputs, beams), jnp.bfloat16)] * 2
-        + [
+        scratch_shapes=[
             pltpu.VMEM((lanes // LANES, sources * size, LANES), jnp.float32),
             pltpu.VMEM((block, beams // LANES, spectra, LANES), jnp.float32),
         ],
         compiler_params=pltpu.CompilerParams(dimension_semantics=("arbitrary",)),
         name="correlate",
-    )(bins, cal_gains.reshape(2, block, RADIX, 1, inputs), beam_delays)
+    )(bins, cal_gains.reshape(2, block, RADIX, 1, inputs), weights)
     return (
         vis.reshape(2, chan_local, inputs, inputs),
         power.reshape(chan_local, spectra, beams),
@@ -443,8 +467,9 @@
     halo = shifted(voltages[:, : (TAPS - 1) * NFFT].astype(jnp.bfloat16), "tm", -1)
     devices = tm_count * chan_count
     if CH % (4 * RADIX * devices) == 0:
+        weights = beam_weights(beam_delays, CH // devices // RADIX)
         bins = exchange(channelize(voltages, halo, devices))
-        return correlate_bins(bins, beam_delays, cal_gains)
+        return correlate_bins(bins, weights, cal_gains)
     half = LANES // 2
     bins = channelize(voltages, halo, half).reshape(RADIX // 2, half, 2, 2, spec_dev, inp_dev)
     plain, mirror = bins[:, :, 0], bins[:, :, 1]

time: 149 us -> 148 us (level)
  waiting for transfers between devices: 32 us -> 5.93 us
  Pallas kernels: 107 us -> 131 us
    pallas_call x0 -> x1, Pallas kernels: none -> 26.1 us  [beam_weights(): pl.pallas_call(weights_kernel, grid=(RADIX,), in_specs=[pl.BlockSpec((bea...]
    ppermute x1, waiting for transfers between devices: 32 us -> 5.93 us  [shifted(): return lax.ppermute(block, axis, route)]
    pallas_call x1, Pallas kernels: 44.1 us -> 42.6 us  [correlate_bins(): pl.pallas_call(correlate_bins_kernel, grid=(RADIX,), in_specs=[pl.BlockSp...]
  transfers between devices with their start and end apart: 1 -> 1, of which waited for: 1 -> 1; matrix products, arithmetic and copies ran while one was open for 2% -> 2% of each run, Pallas kernels for 0% -> 18%
where the time goes in v2:
time: 148 us; the launch traced here: 147 us
  Pallas kernels  131 us (89%)
  waiting for transfers between devices  5.93 us (4%)
  other arithmetic  3.66 us (2%)
  local copies, waits for them, and re-layouts  2.57 us (2%)
  starting transfers between devices  1.92 us (1%)
    pallas_call x1, Pallas kernels, exchange(): pl.pallas_call(exchange_kernel, in_specs=[pl.BlockSpec(memory_space=pl.AN...  50.5 us
    pallas_call x1, Pallas kernels, correlate_bins(): pl.pallas_call(correlate_bins_kernel, grid=(RADIX,), in_specs=[pl.BlockSp...  42.6 us
    pallas_call x1, Pallas kernels, beam_weights(): pl.pallas_call(weights_kernel, grid=(RADIX,), in_specs=[pl.BlockSpec((bea...  26.1 us
    pallas_call x1, Pallas kernels, channelize(): pl.pallas_call(channelize_kernel, out_shape=jax.ShapeDtypeStruct((groups,...  12.4 us
    ppermute x1, waiting for transfers between devices, shifted(): return lax.ppermute(block, axis, route)  5.93 us
  transfers between devices with their start and end apart: 1, of which 1 were waited for; matrix products, arithmetic and copies ran while one was open for 2% of the time, Pallas kernels for 18%

profile of v2, /device:TPU:9, one launch (start us, length us, event | category | flops | bytes accessed | tf_op | source)
XLA Modules:
  0.0 146.9 jit_solution(6672660335089736311)
XLA Ops:
  0.6 0.0 copy-start.1
  0.6 2.1 %slice_convert_fusion = bf16[64,12288]{1,0:T(8,128)(2,1)S(1)} fusion(s32[64,16384]{1,0:T(8,128)} %volt_ref.1), kind=kLoop, calls=%fused_computation | loop fusion | flops 786432 | bytes 4718592 | tf_op jit(solution)/shard_map/convert
  2.7 1.9 %collective-permute-start = (bf16[64,12288]{1,0:T(8,128)(2,1)S(1)}, bf16[64,12288]{1,0:T(8,128)(2,1)S(1)}, u32[]{:S(2)}, u32[]{:S(2)}) collective-permute-start(bf16[64,12288]{1,0:T(8,128)(2,1)S(1)} %slice_convert_fusion), channel_id=1, source_target_pairs={{4,0},{8,4},{12,8},{5,1},{9,5},{13,9},{6,2},{10,6},{14,10},{7,3},{... | collective-permute-start | bytes 4718600 | tf_op jit(solution)/shard_map/ppermute | solution.py:22
  4.7 0.9 fusion.42
  6.3 0.0 copy-done.1
  6.3 1.0 reshape.63.gain_ref
  7.3 0.0 copy-start.2
  7.3 26.1 %beam_weights.1.weight_ref = bf16[32,4,2,256,256]{4,3,2,1,0:T(8,128)(2,1)} custom-call(s32[256,256]{1,0:T(8,128)} %delay_ref.1), custom_call_target="tpu_custom_call" | custom-call | flops 201326592 | bytes 33554432 | tf_op jit(solution)/shard_map/beam_weights/pallas_call | solution.py:261
  33.3 0.6 fusion.15
  34.0 5.9 %collective-permute-done.halo_ref = bf16[64,12288]{1,0:T(8,128)(2,1)S(1)} collective-permute-done((bf16[64,12288]{1,0:T(8,128)(2,1)S(1)}, bf16[64,12288]{1,0:T(8,128)(2,1)S(1)}, u32[]{:S(2)}, u32[]{:S(2)}) %collective-permute-start) | collective-permute-done | bytes 1572896 | tf_op jit(solution)/shard_map/ppermute | solution.py:22
  39.9 0.0 copy-start
  39.9 0.9 broadcast_in_dim.10.window_ref
  40.8 0.0 copy-done.2
  40.8 0.7 jit_solution_.3.twiddle_ref
  41.5 0.0 copy-done
  41.5 12.4 %channelize.1.out_ref = bf16[16,16,16,256]{3,2,1,0:T(8,128)(2,1)} custom-call(s32[64,16384]{1,0:T(8,128)} %volt_ref.1, bf16[64,12288]{1,0:T(8,128)(2,1)} %copy-done, f32[4,8,4096]{2,1,0:T(8,128)} %broadcast_in_dim.10.window_ref, f32[17,2,8,128]{3,2,1,0:T(8,128)} %jit_solution_.3.twiddle_ref, bf16[3,2,256,256]{3,2,1,0:T(8,128)(2,1)} %constant.69.clone.dft_ref), custom_call_target="tpu_custom_call" | custom-call | tf_op jit(solution)/shard_map/channelize/pallas_call | solution.py:149
  53.9 50.5 %exchange.1.bins_ref = bf16[16,16,16,256]{3,2,1,0:T(8,128)(2,1)} custom-call(bf16[16,16,16,256]{3,2,1,0:T(8,128)(2,1)} %channelize.1.out_ref), custom_call_target="tpu_custom_call" | custom-call | tf_op jit(solution)/shard_map/exchange/pallas_call | solution.py:202
  104.3 42.6 %correlate.1 = (bf16[2,4,32,256,256]{4,3,2,1,0:T(8,128)(2,1)}, bf16[4,32,16,256]{3,2,1,0:T(8,128)(2,1)}) custom-call(bf16[16,16,16,256]{3,2,1,0:T(8,128)(2,1)} %exchange.1.bins_ref, f32[2,4,32,1,256]{4,3,2,1,0:T(1,128)} %reshape.63.gain_ref, bf16[32,4,2,256,256]{4,3,2,1,0:T(8,128)(2,1)} %beam_weights.1.weight_ref), custom_call_target="tpu_custom_call" | custom-call | tf_op jit(solution)/shard_map/correlate/pallas_call | solution.py:342
Async XLA Ops:
  0.6 5.7 %copy-start.1 = (f32[2,128,256]{2,1,0:T(8,128)S(1)}, f32[2,128,256]{2,1,0:T(8,128)}, u32[]{:S(2)}) copy-start(f32[2,128,256]{2,1,0:T(8,128)} %param.7) | copy-start | bytes 786436
  2.7 37.2 %collective-permute-start = (bf16[64,12288]{1,0:T(8,128)(2,1)S(1)}, bf16[64,12288]{1,0:T(8,128)(2,1)S(1)}, u32[]{:S(2)}, u32[]{:S(2)}) collective-permute-start(bf16[64,12288]{1,0:T(8,128)(2,1)S(1)} %slice_convert_fusion), channel_id=1, source_target_pairs={{4,0},{8,4},{12,8},{5,1},{9,5},{13,9},{6,2},{10,6},{14,10},{7,3},{... | collective-permute-start | bytes 4718600 | tf_op jit(solution)/shard_map/ppermute | solution.py:22
  7.3 33.6 %copy-start.2 = (f32[17,2,128]{2,1,0:T(2,128)S(1)}, f32[17,2,128]{2,1,0:T(2,128)}, u32[]{:S(2)}) copy-start(f32[17,2,128]{2,1,0:T(2,128)} %constant.68.clone) | copy-start | bytes 52228
  39.9 1.6 %copy-start = (bf16[64,12288]{1,0:T(8,128)(2,1)}, bf16[64,12288]{1,0:T(8,128)(2,1)S(1)}, u32[]{:S(2)}) copy-start(bf16[64,12288]{1,0:T(8,128)(2,1)S(1)} %collective-permute-done.halo_ref) | copy-start | bytes 4718596

commit v3 on v1

--- a/solution.py
+++ b/solution.py
@@ -259,7 +259,7 @@
                 c_re, c_im = c_re * r_re - c_im * r_im, c_re * r_im + c_im * r_re
         return carry
 
-    lax.fori_loop(0, inputs // rows, advance, 0)
+    lax.fori_loop(0, inputs // rows, advance, 0, unroll=True)
 
     received = bins_ref[...].astype(jnp.float32).reshape(sources * size, lanes)
     for part in range(lanes // LANES):
@@ -385,7 +385,7 @@
         cur_im[at, :] = c_im
         return carry
 
-    lax.fori_loop(0, inputs // rows, advance, 0)
+    lax.fori_loop(0, inputs // rows, advance, 0, unroll=True)
 
     for c in range(block):
         a_re = spec_ref[0, c].astype(jnp.float32)

time: 149 us -> 142 us (0.953)
  Pallas kernels: 107 us -> 99.5 us
    pallas_call x1, Pallas kernels: 44.1 us -> 36.6 us  [correlate_bins(): pl.pallas_call(correlate_bins_kernel, grid=(RADIX,), in_specs=[pl.BlockSp...]
where the time goes in v3:
time: 142 us; the launch traced here: 141 us
  Pallas kernels  99.5 us (70%)
  waiting for transfers between devices  32 us (23%)
  other arithmetic  3.66 us (3%)
  local copies, waits for them, and re-layouts  2.54 us (2%)
  starting transfers between devices  1.92 us (1%)
    pallas_call x1, Pallas kernels, exchange(): pl.pallas_call(exchange_kernel, in_specs=[pl.BlockSpec(memory_space=pl.AN...  50.5 us
    pallas_call x1, Pallas kernels, correlate_bins(): pl.pallas_call(correlate_bins_kernel, grid=(RADIX,), in_specs=[pl.BlockSp...  36.6 us
    ppermute x1, waiting for transfers between devices, shifted(): return lax.ppermute(block, axis, route)  32 us
    pallas_call x1, Pallas kernels, channelize(): pl.pallas_call(channelize_kernel, out_shape=jax.ShapeDtypeStruct((groups,...  12.4 us
  transfers between devices with their start and end apart: 1, of which 1 were waited for; matrix products, arithmetic and copies ran while one was open for 2% of the time, Pallas kernels for 0%

profile of v3, /device:TPU:9, one launch (start us, length us, event | category | flops | bytes accessed | tf_op | source)
XLA Modules:
  0.0 140.9 jit_solution(12050398173309754797)
XLA Ops:
  0.6 0.0 copy-start.2
  0.6 0.0 copy-start.1
  0.7 2.1 %slice_convert_fusion = bf16[64,12288]{1,0:T(8,128)(2,1)S(1)} fusion(s32[64,16384]{1,0:T(8,128)} %volt_ref.1), kind=kLoop, calls=%fused_computation | loop fusion | flops 786432 | bytes 4718592 | tf_op jit(solution)/shard_map/convert
  2.7 1.9 %collective-permute-start = (bf16[64,12288]{1,0:T(8,128)(2,1)S(1)}, bf16[64,12288]{1,0:T(8,128)(2,1)S(1)}, u32[]{:S(2)}, u32[]{:S(2)}) collective-permute-start(bf16[64,12288]{1,0:T(8,128)(2,1)S(1)} %slice_convert_fusion), channel_id=1, source_target_pairs={{4,0},{8,4},{12,8},{5,1},{9,5},{13,9},{6,2},{10,6},{14,10},{7,3},{... | collective-permute-start | bytes 4718600 | tf_op jit(solution)/shard_map/ppermute | solution.py:22
  4.7 0.9 fusion.42
  6.3 0.0 copy-done.1
  6.3 1.0 reshape.63.gain_ref
  7.3 0.6 fusion.15
  7.9 32.0 %collective-permute-done.halo_ref = bf16[64,12288]{1,0:T(8,128)(2,1)S(1)} collective-permute-done((bf16[64,12288]{1,0:T(8,128)(2,1)S(1)}, bf16[64,12288]{1,0:T(8,128)(2,1)S(1)}, u32[]{:S(2)}, u32[]{:S(2)}) %collective-permute-start) | collective-permute-done | bytes 1572896 | tf_op jit(solution)/shard_map/ppermute | solution.py:22
  39.9 0.0 copy-start
  39.9 0.9 broadcast_in_dim.10.window_ref
  40.8 0.0 copy-done.2
  40.8 0.7 jit_solution_.3.twiddle_ref
  41.5 0.0 copy-done
  41.5 12.4 %channelize.1.out_ref = bf16[16,16,16,256]{3,2,1,0:T(8,128)(2,1)} custom-call(s32[64,16384]{1,0:T(8,128)} %volt_ref.1, bf16[64,12288]{1,0:T(8,128)(2,1)} %copy-done, f32[4,8,4096]{2,1,0:T(8,128)} %broadcast_in_dim.10.window_ref, f32[17,2,8,128]{3,2,1,0:T(8,128)} %jit_solution_.3.twiddle_ref, bf16[3,2,256,256]{3,2,1,0:T(8,128)(2,1)} %constant.69.clone.dft_ref), custom_call_target="tpu_custom_call" | custom-call | tf_op jit(solution)/shard_map/channelize/pallas_call | solution.py:149
  53.8 50.5 %exchange.1.bins_ref = bf16[16,16,16,256]{3,2,1,0:T(8,128)(2,1)} custom-call(bf16[16,16,16,256]{3,2,1,0:T(8,128)(2,1)} %channelize.1.out_ref), custom_call_target="tpu_custom_call" | custom-call | tf_op jit(solution)/shard_map/exchange/pallas_call | solution.py:202
  104.3 36.6 %correlate.1 = (bf16[2,4,32,256,256]{4,3,2,1,0:T(8,128)(2,1)}, bf16[4,32,16,256]{3,2,1,0:T(8,128)(2,1)}) custom-call(bf16[16,16,16,256]{3,2,1,0:T(8,128)(2,1)} %exchange.1.bins_ref, f32[2,4,32,1,256]{4,3,2,1,0:T(1,128)} %reshape.63.gain_ref, s32[256,256]{1,0:T(8,128)} %delay_ref.1), custom_call_target="tpu_custom_call" | custom-call | tf_op jit(solution)/shard_map/correlate/pallas_call | solution.py:316
Async XLA Ops:
  0.6 40.2 %copy-start.2 = (f32[17,2,128]{2,1,0:T(2,128)S(1)}, f32[17,2,128]{2,1,0:T(2,128)}, u32[]{:S(2)}) copy-start(f32[17,2,128]{2,1,0:T(2,128)} %constant.68.clone) | copy-start | bytes 52228
  0.6 5.7 %copy-start.1 = (f32[2,128,256]{2,1,0:T(8,128)S(1)}, f32[2,128,256]{2,1,0:T(8,128)}, u32[]{:S(2)}) copy-start(f32[2,128,256]{2,1,0:T(8,128)} %param.7) | copy-start | bytes 786436
  2.7 37.2 %collective-permute-start = (bf16[64,12288]{1,0:T(8,128)(2,1)S(1)}, bf16[64,12288]{1,0:T(8,128)(2,1)S(1)}, u32[]{:S(2)}, u32[]{:S(2)}) collective-permute-start(bf16[64,12288]{1,0:T(8,128)(2,1)S(1)} %slice_convert_fusion), channel_id=1, source_target_pairs={{4,0},{8,4},{12,8},{5,1},{9,5},{13,9},{6,2},{10,6},{14,10},{7,3},{... | collective-permute-start | bytes 4718600 | tf_op jit(solution)/shard_map/ppermute | solution.py:22
  39.9 1.5 %copy-start = (bf16[64,12288]{1,0:T(8,128)(2,1)}, bf16[64,12288]{1,0:T(8,128)(2,1)S(1)}, u32[]{:S(2)}) copy-start(bf16[64,12288]{1,0:T(8,128)(2,1)S(1)} %collective-permute-done.halo_ref) | copy-start | bytes 4718596
